TPU v7x, 256 devices: a whole 4x4x8 slice. The times are simulated.
256 devices in a mesh: head: 8 (over z), seq: 32 (over y, x, core).
Axes of the slice: x: 4, y: 4, z: 8, core: 2. Of those that a mesh axis runs over, the one named last changes fastest.
Arguments:
- queries: bfloat16 [4096, 8192], P('seq', 'head'), may hold values from -100 to 100
- keys: bfloat16 [4096, 1024], P('seq', 'head'), may hold values from -5 to 5
- values: bfloat16 [4096, 1024], P('seq', 'head'), may hold values from -6 to 6
- q_tangent: bfloat16 [4096, 8192], P('seq', 'head'), may hold values from -6 to 6
- k_tangent: bfloat16 [4096, 1024], P('seq', 'head'), may hold values from -6 to 6
- v_tangent: bfloat16 [4096, 1024], P('seq', 'head'), may hold values from -6 to 6
- out_grad: bfloat16 [4096, 8192], P('seq', 'head'), may hold values from -6 to 6
- block_order: int32 [32], replicated, may hold values from 0 to 31, each once
Outputs:
- dq_tangent: bfloat16 [4096, 8192], P('seq', 'head')
- dk_tangent: bfloat16 [4096, 1024], P('seq', 'head')
- dv_tangent: bfloat16 [4096, 1024], P('seq', 'head')
- squared_norm: float32 [], replicated
Inputs may be any that keep to these rules, and one draw needn't show every extreme that they name: `block_order`: every value of 0 to 31 appears once.
All inputs are finite; a program needn't handle non-finite values.
Results may differ from a plain program's by a relative error of at most 0.025.
Values may be sent and summed in bfloat16 or wider, within the bound.
A program may use at most 64 MiB of HBM per device.

v0:
```python
import jax
import jax.numpy as jnp
from jax import lax
from jax.sharding import Mesh
from jax.sharding import PartitionSpec as P

HD = 128
G = 8
SEQ = ("seq_0", "seq_1", "seq_2")


neg_fill = -1e30


def sent_to_all(array, axis):
    devices = lax.axis_size(axis)
    return lax.all_to_all(
        jnp.broadcast_to(array[None], (devices, *array.shape)), axis, 0, 0, tiled=True
    )


def joined_along(tiles, dim):
    shape = list(tiles.shape[1:])
    shape[dim] *= tiles.shape[0]
    return jnp.moveaxis(tiles, 0, dim).reshape(shape)


def gather_axes(array, axes, dim):
    far, near = axes
    tiles = sent_to_all(sent_to_all(array, far), near)
    return joined_along(tiles.swapaxes(0, 1).reshape(-1, *array.shape), dim)


def side_by_side(arrays, axis, dim, along):
    ends, at = ([], 0)
    for a in arrays[:-1]:
        at += a.shape[along]
        ends.append(at)
    both = jnp.concatenate(arrays, axis=along)
    return tuple(jnp.split(gather_axes(both, axis, dim), ends, axis=along))


def cut_along(array, dim, devices):
    shape = array.shape
    tiles = array.reshape(*shape[:dim], devices, shape[dim] // devices, *shape[dim + 1 :])
    return jnp.moveaxis(tiles, dim, 0)


def sent_and_summed(array, axis, dim):
    devices = lax.axis_size(axis)
    tiles = lax.all_to_all(cut_along(array, dim, devices), axis, 0, 0, tiled=True)
    return jnp.sum(tiles.astype(jnp.float32), axis=0)


def sum_in_two_steps(array, axes, dim):
    far, near = axes
    own = sent_and_summed(cut_along(array, dim, lax.axis_size(far)), near, dim + 1)
    return jnp.sum(
        lax.all_to_all(own.astype(jnp.bfloat16), far, 0, 0, tiled=True).astype(jnp.float32), axis=0
    )


def sent_together(arrays, axis, dim, along):
    both = jnp.concatenate(arrays, axis=along)
    whole, at, finished = (sum_in_two_steps(both, axis, dim), 0, [])
    for a in arrays:
        finished.append(lax.slice_in_dim(whole, at, at + a.shape[along], axis=along))
        at += a.shape[along]
    return tuple(finished)


def over_copies(array, axis):
    return sent_to_all(array, axis).sum(axis=0)


def over_axes(array, axes):
    far, near = axes
    return over_copies(over_copies(array, near), far)


def body(queries, keys, values, q_tangent, k_tangent, v_tangent, out_grad, block_order):
    tokens = queries.shape[0]
    heads = keys.shape[1] // HD
    scaling = HD ** (-0.5)
    shards = lax.axis_size(SEQ)
    my_index = lax.axis_index(SEQ)
    my_block = block_order[my_index]
    query_pos = my_block * tokens + jnp.arange(tokens, dtype=jnp.int32)
    query_rows = queries.reshape(tokens, heads, G, HD)
    query_tan = q_tangent.reshape(tokens, heads, G, HD)
    grad_rows = out_grad.reshape(tokens, heads, G, HD)

    def block_scores(blocks, key_pos):
        key_blk, val_blk, key_tan, val_tan = [b.reshape(b.shape[0], heads, HD) for b in blocks]
        visible = (key_pos[None, :] <= query_pos[:, None])[None, None]
        s_main = (
            jnp.einsum("thgd,shd->hgts", query_rows, key_blk, preferred_element_type=jnp.float32)
            * scaling
        )
        s_tan = (
            jnp.einsum("thgd,shd->hgts", query_tan, key_blk, preferred_element_type=jnp.float32)
            + jnp.einsum("thgd,shd->hgts", query_rows, key_tan, preferred_element_type=jnp.float32)
        ) * scaling
        d_prob = jnp.einsum(
            "thgd,shd->hgts", grad_rows, val_blk, preferred_element_type=jnp.float32
        )
        d_prob_tan = jnp.einsum(
            "thgd,shd->hgts", grad_rows, val_tan, preferred_element_type=jnp.float32
        )
        return (visible, s_main, s_tan, d_prob, d_prob_tan, key_blk, key_tan)

    def add_stats(row_stats, blocks, key_pos):
        visible, s_main, s_tan, d_prob, d_prob_tan, key_blk, key_tan = block_scores(blocks, key_pos)
        row_max, row_total, tan_sum, grad_sum, cross_sum, extra_sum = row_stats
        new_max = jnp.maximum(row_max, jnp.max(jnp.where(visible, s_main, neg_fill), axis=-1))
        decay = jnp.exp(row_max - new_max)
        expo = jnp.where(visible, jnp.exp(s_main - new_max[..., None]), 0.0)
        return (
            new_max,
            row_total * decay + jnp.sum(expo, axis=-1),
            tan_sum * decay + jnp.sum(expo * s_tan, axis=-1),
            grad_sum * decay + jnp.sum(expo * d_prob, axis=-1),
            cross_sum * decay + jnp.sum(expo * s_tan * d_prob, axis=-1),
            extra_sum * decay + jnp.sum(expo * d_prob_tan, axis=-1),
        )

    def block_grads(finished, blocks, key_pos):
        visible, s_main, s_tan, d_prob, d_prob_tan, key_blk, key_tan = block_scores(blocks, key_pos)
        row_max, row_total, tan_mean, delta, delta_tan = [f[..., None] for f in finished]
        prob = jnp.where(visible, jnp.exp(s_main - row_max), 0.0) / row_total
        prob_tan = prob * (s_tan - tan_mean)
        d_score = prob * (d_prob - delta)
        d_score_tan = prob_tan * (d_prob - delta) + prob * (d_prob_tan - delta_tan)
        prob_tan_b = prob_tan.astype(jnp.bfloat16)
        d_score_b = d_score.astype(jnp.bfloat16)
        d_score_tan_b = d_score_tan.astype(jnp.bfloat16)
        dq_part = (
            jnp.einsum("hgts,shd->thgd", d_score_tan_b, key_blk, preferred_element_type=jnp.float32)
            + jnp.einsum("hgts,shd->thgd", d_score_b, key_tan, preferred_element_type=jnp.float32)
        ) * scaling
        dk_part = (
            jnp.einsum(
                "hgts,thgd->shd", d_score_tan_b, query_rows, preferred_element_type=jnp.float32
            )
            + jnp.einsum("hgts,thgd->shd", d_score_b, query_tan, preferred_element_type=jnp.float32)
        ) * scaling
        dv_part = jnp.einsum(
            "hgts,thgd->shd", prob_tan_b, grad_rows, preferred_element_type=jnp.float32
        )
        key_rows = key_pos.shape[0]
        return (
            dq_part,
            dk_part.reshape(key_rows, heads * HD),
            dv_part.reshape(key_rows, heads * HD),
        )

    row_zero = jnp.zeros((heads, G, tokens), jnp.float32)
    start_stats = (
        jnp.full((heads, G, tokens), neg_fill, jnp.float32),
        row_zero,
        row_zero,
        row_zero,
        row_zero,
        row_zero,
    )
    dq_zero = jnp.zeros((tokens, heads, G, HD), jnp.float32)
    whole = side_by_side((keys, values, k_tangent, v_tangent), (("seq_0", "seq_1"), "seq_2"), 0, 1)
    inverse = (
        jnp.zeros((shards,), jnp.int32).at[block_order].set(jnp.arange(shards, dtype=jnp.int32))
    )
    all_rows = shards * tokens
    ordered = tuple((w.reshape(shards, tokens, -1)[inverse].reshape(all_rows, -1) for w in whole))
    block_rows = min(512, all_rows)
    visits = (my_block * tokens + tokens + block_rows - 1) // block_rows

    def slice_blocks(block_index):
        offset = block_index * block_rows
        pieces = tuple((lax.dynamic_slice_in_dim(o, offset, block_rows, 0) for o in ordered))
        return (pieces, offset + jnp.arange(block_rows, dtype=jnp.int32))

    def stats_turn(block_index, row_stats):
        pieces, key_pos = slice_blocks(block_index)
        return add_stats(row_stats, pieces, key_pos)

    row_max, row_total, tan_sum, grad_sum, cross_sum, extra_sum = lax.fori_loop(
        0, visits, stats_turn, start_stats
    )
    tan_mean = tan_sum / row_total
    delta = grad_sum / row_total
    delta_tan = cross_sum / row_total - tan_mean * delta + extra_sum / row_total
    finished = (row_max, row_total, tan_mean, delta, delta_tan)

    def grad_turn(block_index, carry):
        dq_acc, dk_sorted, dv_sorted = carry
        pieces, key_pos = slice_blocks(block_index)
        dq_part, dk_part, dv_part = block_grads(finished, pieces, key_pos)
        offset = block_index * block_rows
        return (
            dq_acc + dq_part,
            lax.dynamic_update_slice_in_dim(dk_sorted, dk_part, offset, 0),
            lax.dynamic_update_slice_in_dim(dv_sorted, dv_part, offset, 0),
        )

    side_zero = jnp.zeros((all_rows, heads * HD), jnp.float32)
    dq_acc, dk_sorted, dv_sorted = lax.fori_loop(
        0, visits, grad_turn, (dq_zero, side_zero, side_zero)
    )
    dk_local = dk_sorted.reshape(shards, tokens, -1)[block_order].reshape(all_rows, -1)
    dv_local = dv_sorted.reshape(shards, tokens, -1)[block_order].reshape(all_rows, -1)
    dk_total, dv_total = sent_together(
        (dk_local.astype(jnp.bfloat16), dv_local.astype(jnp.bfloat16)),
        (("seq_0", "seq_1"), "seq_2"),
        0,
        1,
    )
    dq_out = dq_acc.reshape(tokens, heads * G * HD).astype(jnp.bfloat16)
    dk_out = dk_total.astype(jnp.bfloat16)
    dv_out = dv_total.astype(jnp.bfloat16)
    dq_wide = dq_out.astype(jnp.float32)
    dk_wide = dk_out.astype(jnp.float32)
    dv_wide = dv_out.astype(jnp.float32)
    local_term = (
        jnp.sum(dq_wide * dq_wide) + jnp.sum(dk_wide * dk_wide) + jnp.sum(dv_wide * dv_wide)
    )
    squared_norm = over_axes(local_term, (("head", "seq_0"), ("seq_1", "seq_2")))
    return (dq_out, dk_out, dv_out, squared_norm)


def solution(mesh):
    torus = Mesh(
        mesh.devices.reshape(mesh.shape["head"], 4, 4, 2), ("head", "seq_0", "seq_1", "seq_2")
    )
    return jax.shard_map(
        body,
        mesh=torus,
        in_specs=(
            P(SEQ, "head"),
            P(SEQ, "head"),
            P(SEQ, "head"),
            P(SEQ, "head"),
            P(SEQ, "head"),
            P(SEQ, "head"),
            P(SEQ, "head"),
            P(),
        ),
        out_specs=(P(SEQ, "head"), P(SEQ, "head"), P(SEQ, "head"), P()),
        check_vma=False,
    )
```

profile of v0, /device:TPU:1, one launch (start us, length us, event | category | flops | bytes accessed | tf_op | source)
XLA Modules:
  0.0 239.0 jit_solution(5662930830812813287)
XLA Ops:
  3.0 7.7 %all-to-all-start = ((bf16[16,128,512]{2,1,0:T(8,128)(2,1)}), bf16[16,128,512]{2,1,0:T(8,128)(2,1)S(1)}, u32[]{:S(2)}, u32[]{:S(2)}) async-start(bf16[16,128,512]{2,1,0:T(8,128)(2,1)} %broadcast_in_dim.87), calls=%async_computation | async-start | bytes 4194304 | tf_op jit(solution)/shard_map/all_to_all | solution.py:17
  13.9 27.3 %all-to-all-done = bf16[16,128,512]{2,1,0:T(8,128)(2,1)S(1)} async-done(((bf16[16,128,512]{2,1,0:T(8,128)(2,1)}), bf16[16,128,512]{2,1,0:T(8,128)(2,1)S(1)}, u32[]{:S(2)}, u32[]{:S(2)}) %all-to-all-start) | async-done | bytes 2097184 | tf_op jit(solution)/shard_map/all_to_all | solution.py:17
  41.7 8.9 %all_to_all.32 = bf16[2,16,128,512]{3,2,1,0:T(8,128)(2,1)S(1)} all-to-all(bf16[2,16,128,512]{3,2,1,0:T(8,128)(2,1)S(1)} %broadcast_in_dim.88), channel_id=1, replica_groups=mesh['head'=8,'seq_0'=4,'seq_1'=4,'seq_2'=2] {'seq_2'}, dimensions={0} | all-to-all | bytes 8388608 | tf_op jit(solution)/shard_map/all_to_all | solution.py:17
  51.0 2.1 fusion.86
  53.1 2.9 %gather_fusion.2 = bf16[32,128,128]{2,1,0:T(8,128)(2,1)} fusion(bf16[32,128,128]{2,1,0:T(8,128)(2,1)} %bitcast.346, s32[1024]{0:T(1024)S(1)} %pad_clamp_fusion.1), kind=kCustom, calls=%fused_computation.2 | custom fusion | bytes 2097280 | tf_op jit(solution)/shard_map/gather | solution.py:172
  56.0 1.7 gather_fusion.3
  58.4 2.0 gather_fusion.1
  60.5 42.9 %while.36 = (s32[]{:T(128)}, f32[1,8,128]{2,1,0:T(8,128)S(1)}, f32[1,8,128]{2,1,0:T(8,128)S(1)}, f32[1,8,128]{2,1,0:T(8,128)S(1)}, f32[1,8,128]{2,1,0:T(8,128)S(...) while((s32[]{:T(128)}, f32[1,8,128]{2,1,0:T(8,128)S(1)}, ...), condition=%wide.region_8.9_spmd.clone, body=%wide.region_1.8_spmd.clone.sunk | while | flops 683219584 | bytes 19211520 | solution.py:185
  62.4 1.9 fusion.139
  67.7 1.9 fusion.139
  73.1 1.9 fusion.139
  78.4 1.9 fusion.139
  83.8 1.9 fusion.139
  89.2 1.9 fusion.139
  94.5 1.9 fusion.139
  99.9 1.9 fusion.139
  105.5 66.1 %while.37 = (s32[]{:T(128)}, f32[128,1,8,128]{0,3,2,1:T(8,128)S(1)}, bf16[4096,128]{1,0:T(8,128)(2,1)}, bf16[4096,128]{1,0:T(8,128)(2,1)}, s32[]{:T(128)}, /*ind...) while((s32[]{:T(128)}, ...), condition=%wide.region_10.11_spmd.clone, body=%wide.region_9.10_spmd.clone.sunk | while | flops 1352204928 | bytes 37778716 | solution.py:205
  108.6 1.6 fusion.165
  116.8 1.6 fusion.165
  141.6 1.6 fusion.165
  149.9 1.6 fusion.165
  166.4 1.6 fusion.165
  171.6 2.9 %gather_fusion.4 = bf16[32,128,128]{2,1,0:T(8,128)(2,1)} fusion(bf16[32,128,128]{2,1,0:T(8,128)(2,1)} %bitcast.340, s32[1024]{0:T(1024)S(1)} %pad_clamp_fusion), kind=kCustom, calls=%fused_computation.4 | custom fusion | bytes 2097280 | tf_op jit(solution)/shard_map/gather | solution.py:208
  174.5 2.9 %gather_fusion.5 = bf16[32,128,128]{2,1,0:T(8,128)(2,1)} fusion(bf16[32,128,128]{2,1,0:T(8,128)(2,1)} %bitcast.18, s32[1024]{0:T(1024)S(1)} %pad_clamp_fusion), kind=kCustom, calls=%fused_computation.5 | custom fusion | bytes 2097280 | tf_op jit(solution)/shard_map/gather | solution.py:209
  177.4 1.8 maximum_bitcast_fusion
  179.4 5.1 %all_to_all.33 = bf16[2,16,128,256]{3,2,1,0:T(8,128)(2,1)S(1)} all-to-all(bf16[2,16,128,256]{3,2,1,0:T(8,128)(2,1)S(1)} %copy.93), channel_id=1, replica_groups=mesh['head'=8,'seq_0'=4,'seq_1'=4,'seq_2'=2] {'seq_2'}, dimensions={0} | all-to-all | bytes 4194304 | tf_op jit(solution)/shard_map/all_to_all | solution.py:51
  184.4 1.7 reduce_sum.121
  186.1 3.7 %all-to-all-start.3 = ((bf16[16,128,256]{2,1,0:T(8,128)(2,1)}), bf16[16,128,256]{2,1,0:T(8,128)(2,1)S(1)}, u32[]{:S(2)}, u32[]{:S(2)}) async-start(bf16[16,128,256]{2,1,0:T(8,128)(2,1)} %reduce_sum.121), calls=%async_computation.3 | async-start | bytes 2097152 | tf_op jit(solution)/shard_map/all_to_all | solution.py:59
  190.5 16.3 %all-to-all-done.3 = bf16[16,128,256]{2,1,0:T(8,128)(2,1)S(1)} async-done(((bf16[16,128,256]{2,1,0:T(8,128)(2,1)}), bf16[16,128,256]{2,1,0:T(8,128)(2,1)S(1)}, u32[]{:S(2)}, u32[]{:S(2)}) %all-to-all-start.3) | async-done | bytes 1048608 | tf_op jit(solution)/shard_map/all_to_all | solution.py:59
  210.3 8.6 %all_to_all.34 = f32[8,1,1]{2,1,0:T(1,128)S(1)} all-to-all(f32[8,1,1]{2,1,0:T(1,128)S(1)} %broadcast_in_dim.93), channel_id=1, replica_groups=mesh['head'=8,'seq_0'=4,'seq_1'=4,'seq_2'=2] {'seq_1','seq_2'}, dimensions={0} | all-to-all | bytes 64 | tf_op jit(solution)/shard_map/all_to_all | solution.py:17
  220.8 9.0 %all-to-all-start.5 = ((f32[32,1,1]{2,1,0:T(1,128)}), f32[32,1,1]{2,1,0:T(1,128)S(1)}, u32[]{:S(2)}, u32[]{:S(2)}) async-start(f32[32,1,1]{2,1,0:T(1,128)} %broadcast_in_dim.94), calls=%async_computation.5 | async-start | bytes 32768 | tf_op jit(solution)/shard_map/all_to_all | solution.py:17
  230.6 7.7 %all-to-all-done.5 = f32[32,1,1]{2,1,0:T(1,128)S(1)} async-done(((f32[32,1,1]{2,1,0:T(1,128)}), f32[32,1,1]{2,1,0:T(1,128)S(1)}, u32[]{:S(2)}, u32[]{:S(2)}) %all-to-all-start.5) | async-done | bytes 160 | tf_op jit(solution)/shard_map/all_to_all | solution.py:17
  (240 shorter events, 98.9 us)
Async XLA Ops:
  3.0 7.8 %copy-start.3 = (s32[32]{0:T(128)S(1)}, s32[32]{0:T(128)}, u32[]{:S(2)}) copy-start(s32[32]{0:T(128)} %param.19) | copy-start | bytes 388
  3.0 9.0 %copy-start = (bf16[128,1024]{1,0:T(8,128)(2,1)S(1)}, bf16[128,1024]{1,0:T(8,128)(2,1)}, u32[]{:S(2)}) copy-start(bf16[128,1024]{1,0:T(8,128)(2,1)} %param.15) | copy-start | bytes 786436
  3.0 9.4 %copy-start.1 = (bf16[128,1024]{1,0:T(8,128)(2,1)S(1)}, bf16[128,1024]{1,0:T(8,128)(2,1)}, u32[]{:S(2)}) copy-start(bf16[128,1024]{1,0:T(8,128)(2,1)} %param.18) | copy-start | bytes 786436
  3.0 38.2 %all-to-all-start = ((bf16[16,128,512]{2,1,0:T(8,128)(2,1)}), bf16[16,128,512]{2,1,0:T(8,128)(2,1)S(1)}, u32[]{:S(2)}, u32[]{:S(2)}) async-start(bf16[16,128,512]{2,1,0:T(8,128)(2,1)} %broadcast_in_dim.87), calls=%async_computation | async-start | bytes 4194304 | tf_op jit(solution)/shard_map/all_to_all | solution.py:17
  10.7 2.0 copy-start.2
  186.1 20.7 %all-to-all-start.3 = ((bf16[16,128,256]{2,1,0:T(8,128)(2,1)}), bf16[16,128,256]{2,1,0:T(8,128)(2,1)S(1)}, u32[]{:S(2)}, u32[]{:S(2)}) async-start(bf16[16,128,256]{2,1,0:T(8,128)(2,1)} %reduce_sum.121), calls=%async_computation.3 | async-start | bytes 2097152 | tf_op jit(solution)/shard_map/all_to_all | solution.py:59
  220.8 17.6 %all-to-all-start.5 = ((f32[32,1,1]{2,1,0:T(1,128)}), f32[32,1,1]{2,1,0:T(1,128)S(1)}, u32[]{:S(2)}, u32[]{:S(2)}) async-start(f32[32,1,1]{2,1,0:T(1,128)} %broadcast_in_dim.94), calls=%async_computation.5 | async-start | bytes 32768 | tf_op jit(solution)/shard_map/all_to_all | solution.py:17
where the time goes:
time: 240 us; the launch traced here: 239 us
  matrix products  103 us (43%)
  waiting for transfers between devices  51.4 us (21%)
  local copies, waits for them, and re-layouts  24.4 us (10%)
  blocking collectives  22.5 us (9%)
  starting transfers between devices  20.4 us (8%)
  other arithmetic  12.2 us (5%)
  between operations  3.6 us (2%)
    all_to_all x2, waiting for transfers between devices, sent_to_all(): lax.all_to_all(jnp.broadcast_to(array[None], (devices, *array.shape)), ax...  35.1 us
    dot_general x16, matrix products, block_scores(): jnp.einsum('thgd,shd->hgts', grad_rows, val_blk, preferred_element_type=j...  25.6 us
    dot_general x16, matrix products, block_scores(): jnp.einsum('thgd,shd->hgts', grad_rows, val_tan, preferred_element_type=j...  25.2 us
    all_to_all x2, blocking collectives, sent_to_all(): lax.all_to_all(jnp.broadcast_to(array[None], (devices, *array.shape)), ax...  17.5 us
    all_to_all x2, starting transfers between devices, sent_to_all(): lax.all_to_all(jnp.broadcast_to(array[None], (devices, *array.shape)), ax...  16.7 us
    all_to_all x1, waiting for transfers between devices, sum_in_two_steps(): lax.all_to_all(own.astype(jnp.bfloat16), far, 0, 0, tiled=True)  16.3 us
    dot_general x16, matrix products, block_scores(): jnp.einsum('thgd,shd->hgts', query_rows, key_tan, preferred_element_type=...  9.84 us
    dot_general x8, matrix products, block_grads(): jnp.einsum('hgts,thgd->shd', d_score_tan_b, query_rows, preferred_element...  8.82 us
  transfers between devices with their start and end apart: 3, of which 3 were waited for; matrix products, arithmetic and copies ran while one was open for 2% of the time, Pallas kernels for 0%

commit v1 on v0

v1 whole, which is shorter than its diff:
```python
import jax
import jax.numpy as jnp
from jax import lax
from jax.experimental import pallas as pl
from jax.experimental.pallas import tpu as pltpu
from jax.sharding import Mesh
from jax.sharding import PartitionSpec as P

HD = 128
G = 8
TOK = 128
ROWS = G * TOK
STEPS = 16
TILE = 256
CHUNK = 16
AXES = ("head", "seq_0", "seq_1", "seq_2")
SEQ = ("seq_0", "seq_1", "seq_2")
SCALE = HD ** -0.5
EXP_SCALE = SCALE * 1.4426950408889634
NEG = -1e30
F32 = jnp.float32
BF16 = jnp.bfloat16
MESH_ID = pl.DeviceIdType.MESH


def mm(a, b):
    return jnp.dot(a, b, preferred_element_type=F32)


def mm_nt(a, b):
    return lax.dot_general(a, b, (((1,), (1,)), ((), ())), preferred_element_type=F32)


def ring(i):
    return i + i // 2 - 2 * (i // 3)


def offsets(p):
    later = (p + 8) // 12
    q = (p - 4) * later
    first = p * (1 - later) + (q // 3) * later
    second = (1 + q % 3) * later
    return ring(first), ring(second)


def kernel(
    order, q_in, k_in, v_in, qt_in, kt_in, vt_in, do_in,
    dq_out, dk_out, dv_out, norm_out,
    kv, w_s, w_st, w_dp, w_dpt, w_qt,
    e_all, st_all, dp_all, dpt_all, max_all,
    run_max, run_sum, run_st, run_dp, run_cross, dq_acc,
    dst_b, ds_b, pt_b,
    pair_send, pair_recv, held, far_recv, near_recv, norm_plane, norm_line,
    g_near_s, g_far_s, g_pair_s, g_own_r, g_other_r,
    r_pair_s, r_pair_r, r_far_s, r_far_r, r_near_s, r_near_r,
    n_plane_s, n_plane_r, n_line_s, n_line_r,
):
    head, y0, x0, c0 = [lax.axis_index(n) for n in AXES]
    mine = order[(y0 * 4 + x0) * 2 + c0]

    def at(plane, a, b):
        x = lax.rem(x0 + a * (1 - plane) + b * plane, 4)
        y = lax.rem(y0 + a * plane + b * (1 - plane), 4)
        return y, x

    def device(a, b):
        y, x = at(c0, a, b)
        return (head, y, x, c0)

    partner = (head, y0, x0, 1 - c0)

    def hidden(plane, p):
        a, b = offsets(p)
        y, x = at(plane, a, b)
        return jnp.where(order[(y * 4 + x) * 2 + plane] < mine, 0.0, NEG)

    def remote(src, dst, s, r, to):
        return pltpu.make_async_remote_copy(
            src_ref=src, dst_ref=dst, send_sem=s, recv_sem=r, device_id=to, device_id_type=MESH_ID
        )

    def in_plane(dy, dx):
        y, x = lax.rem(y0 + dy, 4), lax.rem(x0 + dx, 4)
        return (head, y, x, c0), y * 4 + x

    def in_line(dz, dc):
        z, c = lax.rem(head + dz, 8), lax.rem(c0 + dc, 2)
        return (z, y0, x0, c), z * 2 + c

    far_first = lambda n, m: sorted(
        [(i, j) for i in range(n) for j in range(m) if i or j],
        key=lambda o: -(min(o[0], n - o[0]) + min(o[1], m - o[1])),
    )
    plane_peers, line_peers = far_first(4, 4), far_first(8, 2)

    barrier = pltpu.get_barrier_semaphore()
    for o in plane_peers:
        pl.semaphore_signal(barrier, inc=1, device_id=in_plane(*o)[0], device_id_type=MESH_ID)
    for o in line_peers:
        pl.semaphore_signal(barrier, inc=1, device_id=in_line(*o)[0], device_id_type=MESH_ID)

    kv[0, 0, 0] = k_in[...]
    kv[0, 1, 0] = kt_in[...]
    kv[0, 2, 0] = v_in[...]
    kv[0, 3, 0] = vt_in[...]

    pl.semaphore_wait(barrier, 30)

    back = (0, 2, 1, 3)

    def near_copy(i):
        a = (0, 1, 3, 2)[i]
        slot = back[i]
        return remote(kv.at[0, :, 0], kv.at[slot, :, 0], g_near_s.at[i], g_own_r.at[slot], device(a, 0))

    def far_copy(i, j):
        b = (0, 1, 3, 2)[j]
        slot = 4 + 3 * i + back[j] - 1
        return remote(
            kv.at[i, :, 0], kv.at[slot, :, 0], g_far_s.at[3 * i + j - 1], g_own_r.at[slot], device(0, b)
        )

    def pair_copy(p):
        return remote(kv.at[p, :, 0], kv.at[p, :, 1], g_pair_s.at[p], g_other_r.at[p], partner)

    for i in (1, 2, 3):
        near_copy(i).start()
    pair_copy(0).start()
    for j in (1, 2, 3):
        far_copy(0, j).start()

    for g in range(G):
        c = slice(g * HD, (g + 1) * HD)
        q = q_in[:, c].astype(F32)
        qs = q.T * EXP_SCALE
        hi = qs.astype(BF16)
        w_s[0:HD, c] = hi
        w_s[HD:, c] = (qs - hi.astype(F32)).astype(BF16)
        qt = qt_in[:, c]
        qt = qt.astype(F32).T
        w_st[0:HD, c] = qt.astype(BF16)
        w_qt[:, c] = (qt * (1.0 / SCALE)).astype(BF16)
        w_st[HD:, c] = q.T.astype(BF16)
        do = do_in[:, c]
        dot = do.astype(F32).T
        w_dp[:, c] = dot.astype(BF16)
        dos = dot * (1.0 / SCALE)
        hi = dos.astype(BF16)
        w_dpt[0:HD, c] = hi
        w_dpt[HD:, c] = (dos - hi.astype(F32)).astype(BF16)

    run_max[...] = jnp.full(run_max.shape, NEG, F32)
    for r in (run_sum, run_st, run_dp, run_cross):
        r[...] = jnp.zeros(r.shape, F32)
    dq_acc[...] = jnp.zeros(dq_acc.shape, F32)

    def scores(p, halves, biases, diagonal):
        n = len(halves) * TOK
        k, kt, v, vt = [kv[p, i, pl.ds(halves[0], len(halves))].reshape(n, HD) for i in range(4)]
        kk = jnp.concatenate([k, k], axis=1)
        kkt = jnp.concatenate([k, kt], axis=1)
        vvt = jnp.concatenate([vt, vt], axis=1)
        for t in range(ROWS // TILE):
            c = slice(t * TILE, (t + 1) * TILE)
            s_all = mm(kk, w_s[:, c])
            st_t = mm(kkt, w_st[:, c])
            dp_t = mm(v, w_dp[:, c])
            dpt_t = mm(vvt, w_dpt[:, c])
            new_max = run_max[t]
            parts = []
            for n_at, half in enumerate(halves):
                rows = slice(n_at * TOK, (n_at + 1) * TOK)
                s = s_all[rows]
                if diagonal:
                    key = lax.broadcasted_iota(jnp.int32, (TOK, TILE), 0)
                    tok = lax.rem(lax.broadcasted_iota(jnp.int32, (TOK, TILE), 1), TOK)
                    s = jnp.where(key <= tok, s, NEG)
                s = s.reshape(TOK // 8, 8, TILE)
                top = jnp.max(s, axis=0)
                e = jnp.exp2(s - top[None])
                e_all[p, half, t] = e.reshape(TOK, TILE).astype(BF16)
                st_all[p, half, t] = st_t[rows]
                dp_all[p, half, t] = dp_t[rows]
                dpt_b = dpt_t[rows].astype(BF16)
                dpt_all[p, half, t] = dpt_b
                st = st_t[rows].reshape(TOK // 8, 8, TILE)
                dp = dp_t[rows].reshape(TOK // 8, 8, TILE)
                dpt = dpt_b.astype(F32).reshape(TOK // 8, 8, TILE)
                es = e * st
                top = top if biases[n_at] is None else top + biases[n_at]
                max_all[p, half, t] = top
                new_max = jnp.maximum(new_max, top)
                parts.append((
                    top,
                    jnp.sum(e, axis=0),
                    jnp.sum(es, axis=0),
                    jnp.sum(e * dp, axis=0),
                    jnp.sum(es * dp, axis=0) + jnp.sum(e * dpt, axis=0),
                ))
            decay = jnp.exp2(run_max[t] - new_max)
            run_max[t] = new_max
            weights = [jnp.exp2(part[0] - new_max) for part in parts]
            for i, r in enumerate((run_sum, run_st, run_dp, run_cross)):
                total = r[t] * decay
                for part, weight in zip(parts, weights):
                    total = total + part[i + 1] * weight
                r[t] = total

    scores(0, (0,), (None,), True)
    for i in (1, 2, 3):
        near_copy(back[i]).wait_recv()
        for j in (1, 2, 3):
            far_copy(i, j).start()
        pair_copy(i).start()
    pair_copy(0).wait_recv()
    scores(0, (1,), (hidden(1 - c0, 0),), False)

    def wait_own(p):
        remote(kv.at[0, :, 0], kv.at[p, :, 0], g_pair_s.at[0], g_own_r.at[p], partner).wait_recv()

    def score_step(p, carry):
        @pl.when((p >= 3) & (p < STEPS - 1))
        def _():
            wait_own(p + 1)
            pair_copy(p + 1).start()

        pair_copy(p).wait_recv()
        scores(p, (0, 1), (hidden(c0, p), hidden(1 - c0, p)), False)
        return carry

    lax.fori_loop(1, STEPS, score_step, 0)

    top = jnp.max(run_max[...], axis=1, keepdims=True)
    weight = jnp.exp2(run_max[...] - top)
    sums = [jnp.sum(r[...] * weight, axis=1, keepdims=True) for r in (run_sum, run_st, run_dp, run_cross)]
    inverse = 1.0 / sums[0]
    st_mean = sums[1] * inverse
    delta = sums[2] * inverse
    delta_tan = sums[3] * inverse - st_mean * delta
    for r, value in ((run_max, top), (run_sum, inverse), (run_st, st_mean), (run_dp, delta), (run_cross, delta_tan)):
        r[...] = jnp.broadcast_to(value, r.shape)

    def pair_back(p):
        slot = lax.rem(p, 2)
        return remote(pair_send.at[slot], pair_recv.at[p], r_pair_s.at[slot], r_pair_r.at[p], partner)

    def far_back(p):
        a, b = offsets(p)
        return remote(pair_recv.at[p], far_recv.at[p - 4], r_far_s.at[p - 4], r_far_r.at[p - 4], device(0, b))

    def near_back(p):
        a, b = offsets(p)
        return remote(pair_recv.at[p], near_recv.at[p - 1], r_near_s.at[p - 1], r_near_r.at[p - 1], device(a, 0))

    def summed(p):
        pair_back(p).wait_recv()
        return held[lax.rem(p, 2)] + pair_recv[p].astype(F32)

    def with_far(p, total):
        for j in range(3):
            far_back(4 + 3 * p + j).wait_recv()
            total = total + far_recv[3 * p + j].astype(F32)
        return total

    def send_on(p):
        @pl.when(p >= 4)
        def _():
            pair_recv[p] = summed(p).astype(BF16)
            far_back(p).start()

        @pl.when(p < 4)
        def _():
            pair_recv[p] = with_far(p, summed(p)).astype(BF16)
            near_back(p).start()

    def terms(p):
        def two_tiles(i, carry):
            for t in (2 * i, 2 * i + 1):
                for half in (0, 1):
                    f = jnp.exp2(max_all[p, half, t] - run_max[t]) * run_sum[t]
                    st_mean, delta, delta_tan = run_st[t], run_dp[t], run_cross[t]
                    for at_row in range(0, TOK, CHUNK):
                        from_rows = slice(at_row, at_row + CHUNK)
                        to_rows = slice(half * TOK + at_row, half * TOK + at_row + CHUNK)
                        shape = (CHUNK // 8, 8, TILE)
                        prob = e_all[p, half, t, from_rows].astype(F32).reshape(shape) * f[None]
                        u = st_all[p, half, t, from_rows].reshape(shape) - st_mean[None]
                        v = dp_all[p, half, t, from_rows].reshape(shape) - delta[None]
                        w = dpt_all[p, half, t, from_rows].astype(F32).reshape(shape) - delta_tan[None]
                        pt = prob * u
                        for place, value in ((dst_b, pt * v + prob * w), (ds_b, prob * v), (pt_b, pt)):
                            place[t, to_rows] = value.reshape(CHUNK, TILE).astype(BF16)
            return carry

        lax.fori_loop(0, ROWS // TILE // 2, two_tiles, 0)

    def products(p):
        k = kv[p, 0].reshape(2 * TOK, HD)
        kt = (kv[p, 1].reshape(2 * TOK, HD).astype(F32) * (1.0 / SCALE)).astype(BF16)
        keys = jnp.concatenate([k.T, kt.T], axis=1)
        dk = dv = 0.0
        for t in range(ROWS // TILE):
            c = slice(t * TILE, (t + 1) * TILE)
            dq_acc[t] += mm(keys, jnp.concatenate([dst_b[t], ds_b[t]], axis=0))
            q_both = jnp.concatenate([w_st[HD:, c], w_qt[:, c]], axis=1)
            dk = dk + mm_nt(q_both, jnp.concatenate([dst_b[t], ds_b[t]], axis=1))
            dv = dv + mm_nt(w_dp[:, c], pt_b[t])
        return jnp.concatenate([dk * (SCALE * SCALE), dv * SCALE], axis=0)

    def hand_over(p, both):
        @pl.when(p < STEPS - 2)
        def _():
            pair_back(p).wait_send()

        held[lax.rem(p, 2)] = both[:, :TOK]
        pair_send[lax.rem(p, 2)] = both[:, TOK:].astype(BF16)
        pair_back(p).start()

        @pl.when(p < STEPS - 1)
        def _():
            send_on(p + 1)

    def grad_step(i, carry):
        p = STEPS - 1 - i
        terms(p)
        hand_over(p, products(p))
        return carry

    lax.fori_loop(0, STEPS, grad_step, 0)

    norm = jnp.zeros((8, HD), F32)
    for g in range(G):
        c = slice(g * HD, (g + 1) * HD)
        dq = (dq_acc[g // 2, :, (g % 2) * HD : (g % 2 + 1) * HD] * (SCALE * SCALE)).T.astype(BF16)
        dq_out[:, c] = dq
        wide = dq.astype(F32)
        norm = norm + jnp.sum((wide * wide).reshape(TOK // 8, 8, HD), axis=0)
    total = with_far(0, summed(0))
    for p in (1, 2, 3):
        near_back(p).wait_recv()
        total = total + near_recv[p - 1].astype(F32)
    for out, value in ((dk_out, total[:HD]), (dv_out, total[HD:])):
        value = value.T.astype(BF16)
        out[...] = value
        wide = value.astype(F32)
        norm = norm + jnp.sum((wide * wide).reshape(TOK // 8, 8, HD), axis=0)
    for buffer, place, peers, me, sent, got in (
        (norm_plane, in_plane, plane_peers, y0 * 4 + x0, n_plane_s, n_plane_r),
        (norm_line, in_line, line_peers, head * 2 + c0, n_line_s, n_line_r),
    ):
        buffer[me] = norm
        copies = [
            remote(buffer.at[me], buffer.at[me], sent.at[i], got.at[me], place(*o)[0]) for i, o in enumerate(peers)
        ]
        for copy in copies:
            copy.start()
        for i, o in enumerate(peers):
            to, other = place(*o)
            remote(buffer.at[me], buffer.at[other], sent.at[i], got.at[other], to).wait_recv()
        norm = buffer[0]
        for i in range(1, 16):
            norm = norm + buffer[i]
        for copy in copies:
            copy.wait_send()
    norm_out[0, 0] = jnp.sum(norm)

    for i in (1, 2, 3):
        near_copy(i).wait_send()
    for i in range(4):
        for j in (1, 2, 3):
            far_copy(i, j).wait_send()
    for p in range(STEPS):
        pair_copy(p).wait_send()
    for p in (0, 1):
        pair_back(p).wait_send()
    for p in range(4, STEPS):
        far_back(p).wait_send()
    for p in (1, 2, 3):
        near_back(p).wait_send()


def body(queries, keys, values, q_tangent, k_tangent, v_tangent, out_grad, block_order):
    vmem = pl.BlockSpec(memory_space=pltpu.VMEM)
    stored = lambda dtype: pltpu.VMEM((STEPS, 2, ROWS // TILE, TOK, TILE), dtype)
    row = pltpu.VMEM((ROWS // TILE, 8, TILE), F32)
    sem = lambda n: pltpu.SemaphoreType.DMA((n,))
    dq, dk, dv, norm = pl.pallas_call(
        kernel,
        out_shape=(
            jax.ShapeDtypeStruct((TOK, ROWS), BF16),
            jax.ShapeDtypeStruct((TOK, HD), BF16),
            jax.ShapeDtypeStruct((TOK, HD), BF16),
            jax.ShapeDtypeStruct((1, 1), F32),
        ),
        in_specs=[pl.BlockSpec(memory_space=pltpu.SMEM)] + [vmem] * 7,
        out_specs=(vmem,) * 3 + (pl.BlockSpec(memory_space=pltpu.SMEM),),
        scratch_shapes=[
            pltpu.VMEM((STEPS, 4, 2, TOK, HD), BF16),
            pltpu.VMEM((2 * HD, ROWS), BF16),
            pltpu.VMEM((2 * HD, ROWS), BF16),
            pltpu.VMEM((HD, ROWS), BF16),
            pltpu.VMEM((2 * HD, ROWS), BF16),
            pltpu.VMEM((HD, ROWS), BF16),
            stored(BF16),
            stored(F32),
            stored(F32),
            stored(BF16),
            pltpu.VMEM((STEPS, 2, ROWS // TILE, 8, TILE), F32),
            row, row, row, row, row,
            pltpu.VMEM((ROWS // TILE, HD, TILE), F32),
            pltpu.VMEM((ROWS // TILE, 2 * TOK, TILE), BF16),
            pltpu.VMEM((ROWS // TILE, 2 * TOK, TILE), BF16),
            pltpu.VMEM((ROWS // TILE, 2 * TOK, TILE), BF16),
            pltpu.VMEM((2, 2 * HD, TOK), BF16),
            pltpu.VMEM((STEPS, 2 * HD, TOK), BF16),
            pltpu.VMEM((2, 2 * HD, TOK), F32),
            pltpu.VMEM((12, 2 * HD, TOK), BF16),
            pltpu.VMEM((3, 2 * HD, TOK), BF16),
            pltpu.VMEM((16, 8, HD), F32),
            pltpu.VMEM((16, 8, HD), F32),
            sem(4), sem(12), sem(STEPS), sem(STEPS), sem(STEPS),
            sem(2), sem(STEPS), sem(12), sem(12), sem(3), sem(3),
            sem(15), sem(16), sem(15), sem(16),
        ],
        compiler_params=pltpu.CompilerParams(
            collective_id=0, has_side_effects=True, vmem_limit_bytes=63 * 2**20
        ),
    )(block_order, queries, keys, values, q_tangent, k_tangent, v_tangent, out_grad)
    return dq, dk, dv, norm.reshape(())


def solution(mesh):
    torus = Mesh(mesh.devices.reshape(mesh.shape["head"], 4, 4, 2), AXES)
    split = P(SEQ, "head")
    return jax.shard_map(
        body,
        mesh=torus,
        in_specs=(split,) * 7 + (P(),),
        out_specs=(split,) * 3 + (P(),),
        check_vma=False,
    )
```

time: 240 us -> 77.8 us (0.32)
  matrix products: 103 us -> 0 us
  Pallas kernels: 0 us -> 72.1 us
  waiting for transfers between devices: 51.4 us -> 0 us
  blocking collectives: 22.5 us -> 0 us
  local copies, waits for them, and re-layouts: 24.4 us -> 3.06 us
  starting transfers between devices: 20.4 us -> 0 us
  other arithmetic: 12.2 us -> 0 us
    dot_general x120 -> x0, matrix products: 103 us -> none  [the longest x16 25.6 us: block_scores(): jnp.einsum('thgd,shd->hgts', grad_rows, val_blk, preferred_element_type=j...]
    pallas_call x0 -> x1, Pallas kernels: none -> 72.1 us  [body(): pl.pallas_call(kernel, out_shape=(jax.ShapeDtypeStruct((TOK, ROWS), BF16)...]
    all_to_all x3 -> x0, waiting for transfers between devices: 51.4 us -> none  [the longest x2 35.1 us: sent_to_all(): lax.all_to_all(jnp.broadcast_to(array[None], (devices, *array.shape)), ax...]
    all_to_all x3 -> x0, blocking collectives: 22.5 us -> none  [the longest x2 17.5 us: sent_to_all(): lax.all_to_all(jnp.broadcast_to(array[None], (devices, *array.shape)), ax...]
    all_to_all x3 -> x0, starting transfers between devices: 20.4 us -> none  [the longest x2 16.7 us: sent_to_all(): lax.all_to_all(jnp.broadcast_to(array[None], (devices, *array.shape)), ax...]
    gather x6 -> x0, local copies, waits for them, and re-layouts: 13.2 us -> none  [the longest x4 7.33 us: body(): w.reshape(shards, tokens, -1)[inverse].reshape(all_rows, -1)]
    broadcast_in_dim x13 -> x0, local copies, waits for them, and re-layouts: 5.44 us -> none  [the longest x4 3.28 us: sent_to_all(): jnp.broadcast_to(array[None], (devices, *array.shape))]
    reduce_sum x6 -> x0, other arithmetic: 5.11 us -> none  [the longest x1 1.66 us: sent_and_summed(): return jnp.sum(tiles.astype(jnp.float32), axis=0)]
  transfers between devices with their start and end apart: 3 -> 0, of which waited for: 3 -> 0; matrix products, arithmetic and copies ran while one was open for 2% -> 0% of each run, Pallas kernels for 0% -> 0%
where the time goes in v1:
time: 77.8 us; the launch traced here: 77.6 us
  Pallas kernels  72.1 us (93%)
  local copies, waits for them, and re-layouts  3.06 us (4%)
  between operations  2.41 us (3%)
    pallas_call x1, Pallas kernels, body(): pl.pallas_call(kernel, out_shape=(jax.ShapeDtypeStruct((TOK, ROWS), BF16)...  72.1 us
    unnamed x7, local copies, waits for them, and re-layouts  3.06 us

profile of v1, /device:TPU:1, one launch (start us, length us, event | category | flops | bytes accessed | tf_op | source)
XLA Modules:
  0.0 77.6 jit_solution(14356289703033440530)
XLA Ops:
  0.6 72.1 %shard_map.111 = (bf16[128,1024]{1,0:T(8,128)(2,1)}, bf16[128,128]{1,0:T(8,128)(2,1)}, bf16[128,128]{1,0:T(8,128)(2,1)}, f32[1,1]{1,0:T(1,128)}) custom-call(s32[32]{0:T(128)} %order.1, bf16[128,1024]{1,0:T(8,128)(2,1)} %q_in.1, bf16[128,128]{1,0:T(8,128)(2,1)} %k_in.1, bf16[128,128]{1,0:T(8,128)(2,1)} %v_in.1, bf16[128,1024]{1,0:T(8,128)(2,1)} %qt_in.1, ...), custom_call_target="tpu_custom_call" | custom-call | tf_op jit(solution)/shard_map/pallas_call | solution.py:387
  72.7 0.0 copy-start.1
  72.7 1.7 %copy.16 = bf16[128,1024]{1,0:T(8,128)(2,1)} copy(bf16[128,1024]{1,0:T(8,128)(2,1)} %get-tuple-element.16) | data formatting | bytes 524288
  74.4 0.0 copy-done.1
  74.4 0.0 copy-start
  74.4 0.6 copy.17
  75.0 0.2 copy-done
  75.2 0.6 copy.18
Async XLA Ops:
  72.7 1.7 %copy-start.1 = (bf16[128,128]{1,0:T(8,128)(2,1)S(1)}, bf16[128,128]{1,0:T(8,128)(2,1)}, u32[]{:S(2)}) copy-start(bf16[128,128]{1,0:T(8,128)(2,1)} %get-tuple-element.17) | copy-start | bytes 98308
  74.4 0.8 copy-start

commit v2 on v1

--- a/solution.py
+++ b/solution.py
@@ -12,7 +12,6 @@
 ROWS = G * TOK
 STEPS = 16
 TILE = 256
-CHUNK = 16
 AXES = ("head", "seq_0", "seq_1", "seq_2")
 SEQ = ("seq_0", "seq_1", "seq_2")
 SCALE = HD ** -0.5
@@ -27,10 +26,6 @@
     return jnp.dot(a, b, preferred_element_type=F32)
 
 
-def mm_nt(a, b):
-    return lax.dot_general(a, b, (((1,), (1,)), ((), ())), preferred_element_type=F32)
-
-
 def ring(i):
     return i + i // 2 - 2 * (i // 3)
 
@@ -44,12 +39,12 @@
 
 
 def kernel(
-    order, q_in, k_in, v_in, qt_in, kt_in, vt_in, do_in,
-    dq_out, dk_out, dv_out, norm_out,
-    kv, w_s, w_st, w_dp, w_dpt, w_qt,
+    order, q_hbm, k_in, v_in, qt_hbm, kt_in, vt_in, do_hbm,
+    dq_hbm, dk_hbm, dv_hbm, norm_out,
+    q_in, qt_in, do_in, dq_out, dk_out, dv_out, in_sem, out_sem,
+    kv, w_st, w_dp, q_rows, do_rows,
     e_all, st_all, dp_all, dpt_all, max_all,
     run_max, run_sum, run_st, run_dp, run_cross, dq_acc,
-    dst_b, ds_b, pt_b,
     pair_send, pair_recv, held, far_recv, near_recv, norm_plane, norm_line,
     g_near_s, g_far_s, g_pair_s, g_own_r, g_other_r,
     r_pair_s, r_pair_r, r_far_s, r_far_r, r_near_s, r_near_r,
@@ -79,6 +74,16 @@
             src_ref=src, dst_ref=dst, send_sem=s, recv_sem=r, device_id=to, device_id_type=MESH_ID
         )
 
+    arrivals = [
+        pltpu.make_async_copy(src, dst, in_sem.at[i])
+        for i, (src, dst) in enumerate((
+            (k_in, kv.at[0, 0, 0]), (kt_in, kv.at[0, 1, 0]), (v_in, kv.at[0, 2, 0]), (vt_in, kv.at[0, 3, 0]),
+            (q_hbm, q_in), (qt_hbm, qt_in), (do_hbm, do_in),
+        ))
+    ]
+    for arrival in arrivals:
+        arrival.start()
+
     def in_plane(dy, dx):
         y, x = lax.rem(y0 + dy, 4), lax.rem(x0 + dx, 4)
         return (head, y, x, c0), y * 4 + x
@@ -99,11 +104,25 @@
     for o in line_peers:
         pl.semaphore_signal(barrier, inc=1, device_id=in_line(*o)[0], device_id_type=MESH_ID)
 
-    kv[0, 0, 0] = k_in[...]
-    kv[0, 1, 0] = kt_in[...]
-    kv[0, 2, 0] = v_in[...]
-    kv[0, 3, 0] = vt_in[...]
-
+    for arrival in arrivals:
+        arrival.wait()
+
+    for g in range(G):
+        c = slice(g * HD, (g + 1) * HD)
+        q = q_in[:, c].astype(F32)
+        qt = qt_in[:, c]
+        w_st[0:HD, c] = qt.astype(F32).T.astype(BF16)
+        w_st[HD:, c] = q.T.astype(BF16)
+        do = do_in[:, c]
+        w_dp[:, c] = do.astype(F32).T.astype(BF16)
+        q_rows[g // 2, pl.ds((g % 2) * TOK, TOK), :] = q_in[:, c]
+        q_rows[g // 2, pl.ds(2 * TOK + (g % 2) * TOK, TOK), :] = (qt.astype(F32) * (1.0 / SCALE)).astype(BF16)
+        do_rows[c, :] = do
+
+    run_max[...] = jnp.full(run_max.shape, NEG, F32)
+    for r in (run_sum, run_st, run_dp, run_cross):
+        r[...] = jnp.zeros(r.shape, F32)
+    dq_acc[...] = jnp.zeros(dq_acc.shape, F32)
     pl.semaphore_wait(barrier, 30)
 
     back = (0, 2, 1, 3)
@@ -126,46 +145,18 @@
     for i in (1, 2, 3):
         near_copy(i).start()
     pair_copy(0).start()
-    for j in (1, 2, 3):
-        far_copy(0, j).start()
-
-    for g in range(G):
-        c = slice(g * HD, (g + 1) * HD)
-        q = q_in[:, c].astype(F32)
-        qs = q.T * EXP_SCALE
-        hi = qs.astype(BF16)
-        w_s[0:HD, c] = hi
-        w_s[HD:, c] = (qs - hi.astype(F32)).astype(BF16)
-        qt = qt_in[:, c]
-        qt = qt.astype(F32).T
-        w_st[0:HD, c] = qt.astype(BF16)
-        w_qt[:, c] = (qt * (1.0 / SCALE)).astype(BF16)
-        w_st[HD:, c] = q.T.astype(BF16)
-        do = do_in[:, c]
-        dot = do.astype(F32).T
-        w_dp[:, c] = dot.astype(BF16)
-        dos = dot * (1.0 / SCALE)
-        hi = dos.astype(BF16)
-        w_dpt[0:HD, c] = hi
-        w_dpt[HD:, c] = (dos - hi.astype(F32)).astype(BF16)
-
-    run_max[...] = jnp.full(run_max.shape, NEG, F32)
-    for r in (run_sum, run_st, run_dp, run_cross):
-        r[...] = jnp.zeros(r.shape, F32)
-    dq_acc[...] = jnp.zeros(dq_acc.shape, F32)
 
     def scores(p, halves, biases, diagonal):
         n = len(halves) * TOK
         k, kt, v, vt = [kv[p, i, pl.ds(halves[0], len(halves))].reshape(n, HD) for i in range(4)]
-        kk = jnp.concatenate([k, k], axis=1)
         kkt = jnp.concatenate([k, kt], axis=1)
-        vvt = jnp.concatenate([vt, vt], axis=1)
+        vvt = jnp.concatenate([v, vt], axis=0)
         for t in range(ROWS // TILE):
             c = slice(t * TILE, (t + 1) * TILE)
-            s_all = mm(kk, w_s[:, c])
+            s_all = mm(k, w_st[HD:, c])
             st_t = mm(kkt, w_st[:, c])
-            dp_t = mm(v, w_dp[:, c])
-            dpt_t = mm(vvt, w_dpt[:, c])
+            both = mm(vvt, w_dp[:, c])
+            dp_t, dpt_t = both[:n], both[n:] * (1.0 / SCALE)
             new_max = run_max[t]
             parts = []
             for n_at, half in enumerate(halves):
@@ -177,7 +168,8 @@
                     s = jnp.where(key <= tok, s, NEG)
                 s = s.reshape(TOK // 8, 8, TILE)
                 top = jnp.max(s, axis=0)
-                e = jnp.exp2(s - top[None])
+                e = jnp.exp2((s - top[None]) * EXP_SCALE)
+                top = top * EXP_SCALE
                 e_all[p, half, t] = e.reshape(TOK, TILE).astype(BF16)
                 st_all[p, half, t] = st_t[rows]
                 dp_all[p, half, t] = dp_t[rows]
@@ -208,6 +200,10 @@
 
     scores(0, (0,), (None,), True)
     for i in (1, 2, 3):
+        near_copy(i).wait_send()
+    for j in (1, 2, 3):
+        far_copy(0, j).start()
+    for i in (1, 2, 3):
         near_copy(back[i]).wait_recv()
         for j in (1, 2, 3):
             far_copy(i, j).start()
@@ -273,60 +269,64 @@
             pair_recv[p] = with_far(p, summed(p)).astype(BF16)
             near_back(p).start()
 
-    def terms(p):
-        def two_tiles(i, carry):
-            for t in (2 * i, 2 * i + 1):
-                for half in (0, 1):
-                    f = jnp.exp2(max_all[p, half, t] - run_max[t]) * run_sum[t]
-                    st_mean, delta, delta_tan = run_st[t], run_dp[t], run_cross[t]
-                    for at_row in range(0, TOK, CHUNK):
-                        from_rows = slice(at_row, at_row + CHUNK)
-                        to_rows = slice(half * TOK + at_row, half * TOK + at_row + CHUNK)
-                        shape = (CHUNK // 8, 8, TILE)
-                        prob = e_all[p, half, t, from_rows].astype(F32).reshape(shape) * f[None]
-                        u = st_all[p, half, t, from_rows].reshape(shape) - st_mean[None]
-                        v = dp_all[p, half, t, from_rows].reshape(shape) - delta[None]
-                        w = dpt_all[p, half, t, from_rows].astype(F32).reshape(shape) - delta_tan[None]
-                        pt = prob * u
-                        for place, value in ((dst_b, pt * v + prob * w), (ds_b, prob * v), (pt_b, pt)):
-                            place[t, to_rows] = value.reshape(CHUNK, TILE).astype(BF16)
-            return carry
-
-        lax.fori_loop(0, ROWS // TILE // 2, two_tiles, 0)
-
-    def products(p):
-        k = kv[p, 0].reshape(2 * TOK, HD)
-        kt = (kv[p, 1].reshape(2 * TOK, HD).astype(F32) * (1.0 / SCALE)).astype(BF16)
-        keys = jnp.concatenate([k.T, kt.T], axis=1)
-        dk = dv = 0.0
+    def grad_step(i, carry):
+        p = STEPS - 1 - i
+        dk = jnp.zeros((2 * TOK, HD), F32)
+        dv = jnp.zeros((2 * TOK, HD), F32)
         for t in range(ROWS // TILE):
             c = slice(t * TILE, (t + 1) * TILE)
-            dq_acc[t] += mm(keys, jnp.concatenate([dst_b[t], ds_b[t]], axis=0))
-            q_both = jnp.concatenate([w_st[HD:, c], w_qt[:, c]], axis=1)
-            dk = dk + mm_nt(q_both, jnp.concatenate([dst_b[t], ds_b[t]], axis=1))
-            dv = dv + mm_nt(w_dp[:, c], pt_b[t])
-        return jnp.concatenate([dk * (SCALE * SCALE), dv * SCALE], axis=0)
-
-    def hand_over(p, both):
-        @pl.when(p < STEPS - 2)
+            made = []
+            for half in (0, 1):
+                f = jnp.exp2(max_all[p, half, t] - run_max[t]) * run_sum[t]
+                shape = (TOK // 8, 8, TILE)
+                prob = e_all[p, half, t].astype(F32).reshape(shape) * f[None]
+                u = st_all[p, half, t].reshape(shape) - run_st[t][None]
+                v = dp_all[p, half, t].reshape(shape) - run_dp[t][None]
+                w = dpt_all[p, half, t].astype(F32).reshape(shape) - run_cross[t][None]
+                pt = prob * u
+                made.append([
+                    x.reshape(TOK, TILE).astype(BF16) for x in (pt * v + prob * w, prob * v, pt)
+                ])
+            dst, ds, pt = [jnp.concatenate(x, axis=0) for x in zip(*made)]
+            for half in (0, 1):
+                rows = slice(half * TOK, (half + 1) * TOK)
+                dpt_all[p, half, t] = dst[rows]
+                e_all[p, half, t] = ds[rows]
+            dk = dk + mm(jnp.concatenate([dst, ds], axis=1), q_rows[t])
+            dv = dv + mm(pt, do_rows[c, :])
+        both = jnp.concatenate([dk * (SCALE * SCALE), dv * SCALE], axis=1)
+
+        @pl.when(i >= 2)
         def _():
             pair_back(p).wait_send()
 
-        held[lax.rem(p, 2)] = both[:, :TOK]
-        pair_send[lax.rem(p, 2)] = both[:, TOK:].astype(BF16)
+        held[lax.rem(p, 2)] = both[:TOK]
+        pair_send[lax.rem(p, 2)] = both[TOK:].astype(BF16)
         pair_back(p).start()
 
-        @pl.when(p < STEPS - 1)
+        @pl.when(i >= 1)
         def _():
             send_on(p + 1)
 
-    def grad_step(i, carry):
-        p = STEPS - 1 - i
-        terms(p)
-        hand_over(p, products(p))
         return carry
 
     lax.fori_loop(0, STEPS, grad_step, 0)
+
+    def query_step(i, carry):
+        sides = []
+        for p in (2 * i, 2 * i + 1):
+            k = kv[p, 0].reshape(2 * TOK, HD)
+            kt = (kv[p, 1].reshape(2 * TOK, HD).astype(F32) * (1.0 / SCALE)).astype(BF16)
+            sides += [k.T, kt.T]
+        keys = jnp.concatenate(sides, axis=1)
+        for t in range(ROWS // TILE):
+            terms = []
+            for p in (2 * i, 2 * i + 1):
+                terms += [dpt_all[p, :, t].reshape(2 * TOK, TILE), e_all[p, :, t].reshape(2 * TOK, TILE)]
+            dq_acc[t] += mm(keys, jnp.concatenate(terms, axis=0))
+        return carry
+
+    lax.fori_loop(0, STEPS // 2, query_step, 0)
 
     norm = jnp.zeros((8, HD), F32)
     for g in range(G):
@@ -335,15 +335,23 @@
         dq_out[:, c] = dq
         wide = dq.astype(F32)
         norm = norm + jnp.sum((wide * wide).reshape(TOK // 8, 8, HD), axis=0)
+    departures = [
+        pltpu.make_async_copy(src, dst, out_sem.at[i])
+        for i, (src, dst) in enumerate(((dq_out, dq_hbm), (dk_out, dk_hbm), (dv_out, dv_hbm)))
+    ]
+    departures[0].start()
     total = with_far(0, summed(0))
     for p in (1, 2, 3):
         near_back(p).wait_recv()
         total = total + near_recv[p - 1].astype(F32)
-    for out, value in ((dk_out, total[:HD]), (dv_out, total[HD:])):
-        value = value.T.astype(BF16)
+    for out, value in ((dk_out, total[:, :HD]), (dv_out, total[:, HD:])):
+        value = value.astype(BF16)
         out[...] = value
         wide = value.astype(F32)
         norm = norm + jnp.sum((wide * wide).reshape(TOK // 8, 8, HD), axis=0)
+    departures[1].start()
+    departures[2].start()
+    sends = []
     for buffer, place, peers, me, sent, got in (
         (norm_plane, in_plane, plane_peers, y0 * 4 + x0, n_plane_s, n_plane_r),
         (norm_line, in_line, line_peers, head * 2 + c0, n_line_s, n_line_r),
@@ -360,12 +368,13 @@
         norm = buffer[0]
         for i in range(1, 16):
             norm = norm + buffer[i]
-        for copy in copies:
-            copy.wait_send()
+        sends += copies
     norm_out[0, 0] = jnp.sum(norm)
-
-    for i in (1, 2, 3):
-        near_copy(i).wait_send()
+    for copy in sends:
+        copy.wait_send()
+    for departure in departures:
+        departure.wait()
+
     for i in range(4):
         for j in (1, 2, 3):
             far_copy(i, j).wait_send()
@@ -379,8 +388,13 @@
         near_back(p).wait_send()
 
 
+def hand_on(*refs):
+    for src, dst in zip(refs[:3], refs[3:]):
+        dst[...] = src[...]
+
+
 def body(queries, keys, values, q_tangent, k_tangent, v_tangent, out_grad, block_order):
-    vmem = pl.BlockSpec(memory_space=pltpu.VMEM)
+    hbm = pl.BlockSpec(memory_space=pl.ANY)
     stored = lambda dtype: pltpu.VMEM((STEPS, 2, ROWS // TILE, TOK, TILE), dtype)
     row = pltpu.VMEM((ROWS // TILE, 8, TILE), F32)
     sem = lambda n: pltpu.SemaphoreType.DMA((n,))
@@ -392,15 +406,21 @@
             jax.ShapeDtypeStruct((TOK, HD), BF16),
             jax.ShapeDtypeStruct((1, 1), F32),
         ),
-        in_specs=[pl.BlockSpec(memory_space=pltpu.SMEM)] + [vmem] * 7,
-        out_specs=(vmem,) * 3 + (pl.BlockSpec(memory_space=pltpu.SMEM),),
+        in_specs=[pl.BlockSpec(memory_space=pltpu.SMEM)] + [hbm] * 7,
+        out_specs=(hbm,) * 3 + (pl.BlockSpec(memory_space=pltpu.SMEM),),
         scratch_shapes=[
+            pltpu.VMEM((TOK, ROWS), BF16),
+            pltpu.VMEM((TOK, ROWS), BF16),
+            pltpu.VMEM((TOK, ROWS), BF16),
+            pltpu.VMEM((TOK, ROWS), BF16),
+            pltpu.VMEM((TOK, HD), BF16),
+            pltpu.VMEM((TOK, HD), BF16),
+            sem(7), sem(3),
             pltpu.VMEM((STEPS, 4, 2, TOK, HD), BF16),
             pltpu.VMEM((2 * HD, ROWS), BF16),
-            pltpu.VMEM((2 * HD, ROWS), BF16),
             pltpu.VMEM((HD, ROWS), BF16),
-            pltpu.VMEM((2 * HD, ROWS), BF16),
-            pltpu.VMEM((HD, ROWS), BF16),
+            pltpu.VMEM((G // 2, 4 * TOK, HD), BF16),
+            pltpu.VMEM((ROWS, HD), BF16),
             stored(BF16),
             stored(F32),
             stored(F32),
@@ -408,14 +428,11 @@
             pltpu.VMEM((STEPS, 2, ROWS // TILE, 8, TILE), F32),
             row, row, row, row, row,
             pltpu.VMEM((ROWS // TILE, HD, TILE), F32),
-            pltpu.VMEM((ROWS // TILE, 2 * TOK, TILE), BF16),
-            pltpu.VMEM((ROWS // TILE, 2 * TOK, TILE), BF16),
-            pltpu.VMEM((ROWS // TILE, 2 * TOK, TILE), BF16),
-            pltpu.VMEM((2, 2 * HD, TOK), BF16),
-            pltpu.VMEM((STEPS, 2 * HD, TOK), BF16),
-            pltpu.VMEM((2, 2 * HD, TOK), F32),
-            pltpu.VMEM((12, 2 * HD, TOK), BF16),
-            pltpu.VMEM((3, 2 * HD, TOK), BF16),
+            pltpu.VMEM((2, TOK, 2 * HD), BF16),
+            pltpu.VMEM((STEPS, TOK, 2 * HD), BF16),
+            pltpu.VMEM((2, TOK, 2 * HD), F32),
+            pltpu.VMEM((12, TOK, 2 * HD), BF16),
+            pltpu.VMEM((3, TOK, 2 * HD), BF16),
             pltpu.VMEM((16, 8, HD), F32),
             pltpu.VMEM((16, 8, HD), F32),
             sem(4), sem(12), sem(STEPS), sem(STEPS), sem(STEPS),
@@ -426,6 +443,13 @@
             collective_id=0, has_side_effects=True, vmem_limit_bytes=63 * 2**20
         ),
     )(block_order, queries, keys, values, q_tangent, k_tangent, v_tangent, out_grad)
+    vmem = pl.BlockSpec(memory_space=pltpu.VMEM)
+    dq, dk, dv = pl.pallas_call(
+        hand_on,
+        out_shape=tuple(jax.ShapeDtypeStruct(x.shape, x.dtype) for x in (dq, dk, dv)),
+        in_specs=[vmem] * 3,
+        out_specs=(vmem,) * 3,
+    )(dq, dk, dv)
     return dq, dk, dv, norm.reshape(())
 
 

time: 77.8 us -> 67.7 us (0.87)
  Pallas kernels: 72.1 us -> 65.1 us
  local copies, waits for them, and re-layouts: 3.06 us -> 0 us
    pallas_call x1, Pallas kernels: 72.1 us -> 63.4 us  [body(): pl.pallas_call(kernel, out_shape=(jax.ShapeDtypeStruct((TOK, ROWS), BF16)...]
    unnamed x7 -> x0, local copies, waits for them, and re-layouts: 3.06 us -> none
    pallas_call x0 -> x1, Pallas kernels: none -> 1.7 us  [body(): pl.pallas_call(hand_on, out_shape=tuple((jax.ShapeDtypeStruct(x.shape, x....]
where the time goes in v2:
time: 67.7 us; the launch traced here: 67.5 us
  Pallas kernels  65.1 us (96%)
  between operations  2.4 us (4%)
    pallas_call x1, Pallas kernels, body(): pl.pallas_call(kernel, out_shape=(jax.ShapeDtypeStruct((TOK, ROWS), BF16)...  63.4 us
    pallas_call x1, Pallas kernels, body(): pl.pallas_call(hand_on, out_shape=tuple((jax.ShapeDtypeStruct(x.shape, x....  1.7 us

profile of v2, /device:TPU:1, one launch (start us, length us, event | category | flops | bytes accessed | tf_op | source)
XLA Modules:
  0.0 67.5 jit_solution(3680649846007571282)
XLA Ops:
  0.6 63.4 %shard_map.111 = (bf16[128,1024]{1,0:T(8,128)(2,1)}, bf16[128,128]{1,0:T(8,128)(2,1)}, bf16[128,128]{1,0:T(8,128)(2,1)}, f32[1,1]{1,0:T(1,128)}) custom-call(s32[32]{0:T(128)} %order.1, bf16[128,1024]{1,0:T(8,128)(2,1)} %q_hbm.1, bf16[128,128]{1,0:T(8,128)(2,1)} %k_in.1, bf16[128,128]{1,0:T(8,128)(2,1)} %v_in.1, bf16[128,1024]{1,0:T(8,128)(2,1)} %qt_hbm.1, ...), custom_call_target="tpu_custom_call" | custom-call | tf_op jit(solution)/shard_map/pallas_call | solution.py:401
  64.1 1.7 %shard_map.112 = (bf16[128,1024]{1,0:T(8,128)(2,1)}, bf16[128,128]{1,0:T(8,128)(2,1)}, bf16[128,128]{1,0:T(8,128)(2,1)}) custom-call(bf16[128,1024]{1,0:T(8,128)(2,1)} %get-tuple-element.11.refs_0_, bf16[128,128]{1,0:T(8,128)(2,1)} %get-tuple-element.12.refs_1_, bf16[128,128]{1,0:T(8,128)(2,1)} %get-tuple-element.13.refs_2_), custom_call_target="tpu_custom_call" | custom-call | tf_op jit(solution)/shard_map/pallas_call | solution.py:447
